TPU v7x, 256 devices: a whole 4x4x8 slice. The times are simulated.
256 devices in a mesh: sub: 16 (over z, core), dom: 16 (over y, x).
Axes of the slice: x: 4, y: 4, z: 8, core: 2. Of those that a mesh axis runs over, the one named last changes fastest.
Arguments:
- start_vectors: float32 [16, 3, 64, 16, 16, 128], P('sub', None, None, 'dom'), may hold values from -6 to 6
- face_x: float32 [16, 16, 16, 128], P('sub', 'dom'), may hold values from 0.1 to 10
- face_y: float32 [16, 16, 16, 128], P('sub', 'dom'), may hold values from 0.1 to 10
- face_z: float32 [16, 16, 16, 128], P('sub', 'dom'), may hold values from 0.1 to 10
- masses: float32 [16, 16, 16, 128], P('sub', 'dom'), may hold values from 0.5 to 2
- active: int32 [16], P('sub'), may hold values from 8 to 16, as said below
Outputs:
- deflation: bfloat16 [16, 3, 64, 16, 16, 128], P('sub', None, None, 'dom')
- coarse_diag: float32 [16, 64, 64], P('sub')
- coarse_off: float32 [16, 64, 64], P('sub')
Inputs may be any that keep to these rules, and one draw needn't show every extreme that they name: `active`: some subdomain has all 16 planes.
All inputs are finite; a program needn't handle non-finite values.
Results may differ from a plain program's by a relative error of at most 0.001.
Values sent between devices are 32-bit elements; how exact they have to be, the bound alone decides.
No kernel may reach another device: no remote copies, remote signals or barrier semaphores. Data moves between devices by JAX's collectives and lax.ppermute only.
A program may use at most 64 MiB of HBM per device.

v0:
```python
import jax
import jax.numpy as jnp
from jax import lax
from jax.sharding import PartitionSpec as P

OV = 4
STEPS = 2


def from_behind(value, axis, steps):
    count = lax.axis_size(axis)
    leading, last = (max(0, -steps), min(count, count - steps))
    return lax.ppermute(value, axis, [(source, source + steps) for source in range(leading, last)])


def with_halo(cells, sides, width):
    for axis, dim in sides:
        count = lax.axis_size(axis)
        ends = count - 1
        head = lax.slice_in_dim(cells, 0, width, axis=dim)
        tail = lax.slice_in_dim(cells, cells.shape[dim] - width, cells.shape[dim], axis=dim)
        cells = jnp.concatenate(
            [
                lax.ppermute(tail, axis, [(i, (i + 1) % count) for i in range(ends)]),
                cells,
                lax.ppermute(head, axis, [((i + 1) % count, i) for i in range(ends)]),
            ],
            axis=dim,
        )
    return cells


def gram_of(left, right):
    return jnp.einsum("ckyxz,clyxz->kl", left, right, precision=lax.Precision.HIGHEST)


def mix_cols(values, matrix):
    return jnp.einsum("ckyxz,kl->clyxz", values, matrix, precision=lax.Precision.HIGHEST)


def inverse_factor(gram_b):
    factor = jnp.linalg.cholesky(gram_b)
    identity = jnp.eye(gram_b.shape[0], dtype=jnp.float32)
    return lax.linalg.triangular_solve(factor, identity, left_side=True, lower=True)


def face_terms(values, weights, along):
    length = values.shape[along]
    head_part = lax.slice_in_dim(values, 0, length - 1, axis=along)
    tail_part = lax.slice_in_dim(values, 1, length, axis=along)
    fluxes = lax.slice_in_dim(weights, 0, length - 1, axis=along - 2)[None, None] * (
        head_part - tail_part
    )
    pad_after = [(0, 0)] * 5
    pad_after[along] = (0, 1)
    pad_before = [(0, 0)] * 5
    pad_before[along] = (1, 0)
    return jnp.pad(fluxes, pad_after) - jnp.pad(fluxes, pad_before)


def lower_faces(weights, along):
    length = weights.shape[along]
    widths = [(0, 0)] * 3
    widths[along] = (1, 0)
    return jnp.pad(lax.slice_in_dim(weights, 0, length - 1, axis=along), widths)


def on_device(start_vectors, face_x, face_y, face_z, masses, active):
    start = start_vectors[0]
    own_x = face_x[0]
    own_y = face_y[0]
    own_z = face_z[0]
    own_mass = masses[0]
    active_now = active[0]
    rows_local = own_y.shape[0]
    planes_all = own_y.shape[1]
    depth_all = own_y.shape[2]
    rows_total = rows_local * lax.axis_size("dom")
    row_index = lax.axis_index("dom") * rows_local + jnp.arange(rows_local, dtype=jnp.int32)
    plane_index = jnp.arange(planes_all, dtype=jnp.int32)
    depth_index = jnp.arange(depth_all, dtype=jnp.int32)
    inside = (plane_index < active_now)[None, :, None]
    keep_x = (plane_index + 1 < active_now)[None, :, None]
    keep_y = inside & (row_index + 1 < rows_total)[:, None, None]
    keep_z = inside & (depth_index + 1 < depth_all)[None, None, :]
    live_x = own_x * keep_x.astype(jnp.float32)
    live_y = own_y * keep_y.astype(jnp.float32)
    live_z = own_z * keep_z.astype(jnp.float32)
    below_row = from_behind(live_y, "dom", 1)
    lower_y = jnp.concatenate([below_row, live_y[:-1]], axis=0)
    diagonal = (
        live_x
        + lower_faces(live_x, 1)
        + live_y
        + lower_y
        + live_z
        + lower_faces(live_z, 2)
        + own_mass
    )
    unity = jnp.clip(
        jnp.minimum(plane_index + 1, active_now - plane_index).astype(jnp.float32) / (OV + 1),
        0.0,
        1.0,
    )[None, :, None]
    b_weight = (own_mass * unity * unity)[None, None]

    def operate(values):
        padded = with_halo(values, (("dom", 2),), 1)
        result = live_y[None, None] * (values - padded[:, :, 2:]) + lower_y[None, None] * (
            values - padded[:, :, :-2]
        )
        return result + face_terms(values, live_x, 3) + face_terms(values, live_z, 4)

    vectors = start * inside.astype(jnp.float32)[None, None]

    def normalize(values):
        gram_b = lax.psum(gram_of(values, b_weight * values), "dom")
        return mix_cols(values, inverse_factor(gram_b).T)

    for repeat in range(STEPS):
        ortho = normalize(vectors)
        image = operate(ortho)
        rayleigh = lax.psum(gram_of(ortho, image), "dom")
        residual = image - mix_cols(b_weight * ortho, rayleigh)
        vectors = ortho - 0.5 * residual / diagonal[None, None]
    deflate = unity[None, None] * normalize(vectors)
    image = operate(deflate)
    planes = lax.dynamic_slice_in_dim(image, active_now - OV, OV, axis=3)
    neighbour = from_behind(planes, "sub", 1)
    coarse_diag, coarse_off = lax.psum(
        (gram_of(deflate, image), gram_of(deflate[:, :, :, :OV], neighbour)), "dom"
    )
    return (deflate.astype(jnp.bfloat16)[None], coarse_diag[None], coarse_off[None])


def solution(mesh):
    placed = (
        P("sub", None, None, "dom", None, None),
        P("sub", "dom", None, None),
        P("sub", "dom", None, None),
        P("sub", "dom", None, None),
        P("sub", "dom", None, None),
        P("sub"),
    )
    return jax.shard_map(
        on_device,
        mesh=mesh,
        in_specs=placed,
        out_specs=(
            P("sub", None, None, "dom", None, None),
            P("sub", None, None),
            P("sub", None, None),
        ),
        check_vma=False,
    )
```

profile of v0, /device:TPU:128, one launch (start us, length us, event | category | flops | bytes accessed | tf_op | source)
XLA Modules:
  0.0 587.5 jit_solution(13905922017482201523)
XLA Ops:
  1.3 0.8 fusion.104
  2.1 1.7 bitcast_multiply_fusion.1
  3.8 0.1 copy-done
  4.0 0.3 multiply_bitcast_fusion.1
  4.3 2.2 fusion.50
  6.5 74.6 %psum.49 = f32[64,64]{0,1:T(8,128)S(1)} all-reduce(f32[64,64]{0,1:T(8,128)S(1)} %fusion.50), channel_id=1, replica_groups=mesh['sub'=16,'dom'=16] {'dom'}, use_global_device_ids=true, to_apply=%region_0.1 | all-reduce | flops 4096 | bytes 32768 | tf_op jit(solution)/shard_map/psum | solution.py:117
  81.1 0.1 copy.12
  81.2 5.8 cholesky.59
  87.1 0.6 compare_reduce_fusion.2
  87.7 0.7 fusion.88
  88.4 4.9 custom-call.7
  93.3 0.3 convolution_bitcast_fusion.3
  93.6 1.9 fusion.32
  95.4 1.3 collective-permute-start
  96.7 5.7 collective-permute-start.2
  102.5 1.3 collective-permute-start.1
  104.0 0.2 fusion.49
  104.2 0.5 fusion.2
  104.8 16.0 %collective-permute-done.1 = f32[1,16,128]{2,1,0:T(8,128)S(1)} collective-permute-done((f32[1,16,128]{2,1,0:T(8,128)S(1)}, f32[1,16,128]{2,1,0:T(8,128)S(1)}, u32[]{:S(2)}, u32[]{:S(2)}) %collective-permute-start.1) | collective-permute-done | bytes 8224 | tf_op jit(solution)/shard_map/ppermute | solution.py:13
  120.8 0.1 fusion.103
  120.9 4.1 fusion.65
  125.0 71.9 %psum.50 = f32[64,64]{0,1:T(8,128)S(1)} all-reduce(f32[64,64]{0,1:T(8,128)S(1)} %fusion.65), channel_id=1, replica_groups=mesh['sub'=16,'dom'=16] {'dom'}, use_global_device_ids=true, to_apply=%region_3.6 | all-reduce | flops 4096 | bytes 32768 | tf_op jit(solution)/shard_map/psum | solution.py:123
  196.9 6.0 %fusion.12 = f32[3,64,1,16,128]{4,1,3,0,2:T(8,128)S(1)} fusion(f32[16,128]{1,0:T(8,128)S(1)} %fusion.103, f32[16,128]{1,0:T(8,128)S(1)} %fusion.104, f32[64,64]{0,1:T(8,128)S(1)} %psum.50, f32[64,3,16,128]{3,0,2,1:T(8,128)S(1)} %fusion.32, f32[3,64,1,16,127]{4,1,3,0,2:T(8,128)} %copy-done.1, f32[3,64,1,15,128]{4,1,3,0,2:T(8,128)} %copy-done.3, ...), kind=kOutput, calls=%fused_computation.17 | convolution fusion | flops 307494912 | bytes 9375744 | tf_op jit(solution)/shard_map/ckyxz,kl->clyxz/dot_general | solution.py:38
  202.9 1.4 fusion.55
  204.4 69.5 %psum.51 = f32[64,64]{0,1:T(8,128)S(1)} all-reduce(f32[64,64]{0,1:T(8,128)S(1)} %fusion.55), channel_id=1, replica_groups=mesh['sub'=16,'dom'=16] {'dom'}, use_global_device_ids=true, to_apply=%region_4.7 | all-reduce | flops 4096 | bytes 32768 | tf_op jit(solution)/shard_map/psum | solution.py:117
  273.9 0.1 copy.15
  274.0 5.8 cholesky.70
  279.9 0.6 compare_reduce_fusion.1
  280.5 0.7 fusion.89
  281.2 4.9 custom-call.8
  286.1 0.3 convolution_bitcast_fusion.2
  286.4 1.5 fusion.26
  287.9 1.3 collective-permute-start.3
  289.2 4.6 collective-permute-start.4
  293.8 0.2 fusion.48
  294.0 0.5 fusion.1
  294.5 15.8 %collective-permute-done.3 = f32[3,64,1,16,128]{4,1,3,0,2:T(8,128)S(1)} collective-permute-done((f32[3,64,1,16,128]{4,1,3,0,2:T(8,128)S(1)}, f32[3,64,1,16,128]{4,1,3,0,2:T(8,128)S(1)}, u32[]{:S(2)}, u32[]{:S(2)}) %collective-permute-start.3) | collective-permute-done | bytes 1572896 | tf_op jit(solution)/shard_map/ppermute | solution.py:26
  310.3 1.5 collective-permute-done.4
  311.9 1.1 copy-done.7
  313.0 2.1 fusion.70
  315.1 71.9 %psum.52 = f32[64,64]{0,1:T(8,128)S(1)} all-reduce(f32[64,64]{0,1:T(8,128)S(1)} %fusion.70), channel_id=1, replica_groups=mesh['sub'=16,'dom'=16] {'dom'}, use_global_device_ids=true, to_apply=%region_5.8 | all-reduce | flops 4096 | bytes 32768 | tf_op jit(solution)/shard_map/psum | solution.py:123
  387.0 5.8 fusion.7
  392.8 1.4 fusion.60
  394.3 69.5 %psum.53 = f32[64,64]{0,1:T(8,128)S(1)} all-reduce(f32[64,64]{0,1:T(8,128)S(1)} %fusion.60), channel_id=1, replica_groups=mesh['sub'=16,'dom'=16] {'dom'}, use_global_device_ids=true, to_apply=%region_6.9 | all-reduce | flops 4096 | bytes 32768 | tf_op jit(solution)/shard_map/psum | solution.py:117
  463.9 5.8 cholesky.81
  469.8 0.6 compare_reduce_fusion
  470.4 0.7 fusion.90
  471.1 4.9 custom-call.9
  476.0 0.3 convolution_bitcast_fusion.1
  476.2 1.5 bitcast_multiply_fusion
  477.8 1.3 collective-permute-start.5
  479.1 5.7 collective-permute-start.6
  484.8 0.2 fusion.47
  484.9 0.5 fusion
  485.4 14.6 %collective-permute-done.5 = f32[3,64,1,16,128]{4,1,3,0,2:T(8,128)S(1)} collective-permute-done((f32[3,64,1,16,128]{4,1,3,0,2:T(8,128)S(1)}, f32[3,64,1,16,128]{4,1,3,0,2:T(8,128)S(1)}, u32[]{:S(2)}, u32[]{:S(2)}) %collective-permute-start.5) | collective-permute-done | bytes 1572896 | tf_op jit(solution)/shard_map/ppermute | solution.py:26
  500.1 1.5 collective-permute-done.6
  501.5 2.5 subtract_add_fusion
  504.1 1.9 collective-permute-start.7
  506.0 0.1 convert_bitcast_fusion
  506.1 1.4 copy.18
  507.5 1.4 fusion.75
  508.9 5.4 collective-permute-done.7
  514.4 0.5 convolution_bitcast_fusion
  514.8 72.7 %all-reduce.14 = (f32[1,64,64]{2,1,0:T(8,128)}, f32[1,64,64]{2,1,0:T(8,128)}) all-reduce(f32[1,64,64]{2,1,0:T(8,128)S(1)} %fusion.75, f32[1,64,64]{2,1,0:T(8,128)S(1)} %convolution_bitcast_fusion), channel_id=1, replica_groups=mesh['sub'=16,'dom'=16] {'dom'}, use_global_device_ids=true, to_apply=%region_7.10 | all-reduce | flops 8192 | bytes 65536 | tf_op jit(solution)/shard_map/psum | solution.py:130
  (43 shorter events, 0.6 us)
Async XLA Ops:
  2.1 1.9 copy-start
  93.5 8.9 %copy-start.8 = (f32[1,1,16,128]{3,2,1,0:T(8,128)S(1)}, f32[1,1,16,128]{3,2,1,0:T(8,128)}, u32[]{:S(2)}) copy-start(f32[1,1,16,128]{3,2,1,0:T(8,128)} %param.11) | copy-start | bytes 24580
  93.5 10.3 %copy-start.10 = (f32[1,1,16,128]{3,2,1,0:T(8,128)S(1)}, f32[1,1,16,128]{3,2,1,0:T(8,128)}, u32[]{:S(2)}) copy-start(f32[1,1,16,128]{3,2,1,0:T(8,128)} %param.12) | copy-start | bytes 24580
  93.6 10.4 %copy-start.11 = (f32[1,1,16,128]{3,2,1,0:T(8,128)S(1)}, f32[1,1,16,128]{3,2,1,0:T(8,128)}, u32[]{:S(2)}) copy-start(f32[1,1,16,128]{3,2,1,0:T(8,128)} %param.10) | copy-start | bytes 24580
  95.4 25.4 %collective-permute-start = (f32[3,64,1,16,128]{4,1,3,0,2:T(8,128)S(1)}, f32[3,64,1,16,128]{4,1,3,0,2:T(8,128)S(1)}, u32[]{:S(2)}, u32[]{:S(2)}) collective-permute-start(f32[3,64,1,16,128]{4,1,3,0,2:T(8,128)S(1)} %bitcast.253), channel_id=1, source_target_pairs={{1,0},{2,1},{3,2},{4,3},{5,4},{6,5},{7,6},{8,7},{9,8},{10,9},{11,1... | collective-permute-start | bytes 4718600 | tf_op jit(solution)/shard_map/ppermute | solution.py:26
  96.7 24.1 %collective-permute-start.2 = (f32[3,64,1,16,128]{4,1,3,0,2:T(8,128)S(1)}, f32[3,64,1,16,128]{4,1,3,0,2:T(8,128)}, u32[]{:S(2)}, u32[]{:S(2)}) collective-permute-start(f32[3,64,1,16,128]{4,1,3,0,2:T(8,128)S(1)} %bitcast.254), channel_id=1, source_target_pairs={{0,1},{1,2},{2,3},{3,4},{4,5},{5,6},{6,7},{7,8},{8,9},{9,10},{10,1... | collective-permute-start | bytes 4718600 | tf_op jit(solution)/shard_map/ppermute | solution.py:24
  102.5 18.2 %collective-permute-start.1 = (f32[1,16,128]{2,1,0:T(8,128)S(1)}, f32[1,16,128]{2,1,0:T(8,128)S(1)}, u32[]{:S(2)}, u32[]{:S(2)}) collective-permute-start(f32[1,16,128]{2,1,0:T(8,128)S(1)} %bitcast_multiply_fusion.3), channel_id=1, source_target_pairs={{0,1},{1,2},{2,3},{3,4},{4,5},{5,6},{6,7},{7,8},{8,9},{9,10},{10,1... | collective-permute-start | bytes 24584 | tf_op jit(solution)/shard_map/ppermute | solution.py:13
  104.2 16.7 %copy-start.3 = (f32[3,64,1,15,128]{4,1,3,0,2:T(8,128)}, f32[3,64,1,15,128]{4,1,3,0,2:T(8,128)S(1)}, u32[]{:S(2)}) copy-start(f32[3,64,1,15,128]{4,1,3,0,2:T(8,128)S(1)} %fusion.49) | copy-start | bytes 4423684
  104.2 16.6 %copy-start.9 = (f32[1,1,16,128]{3,2,1,0:T(8,128)S(1)}, f32[1,1,16,128]{3,2,1,0:T(8,128)}, u32[]{:S(2)}) copy-start(f32[1,1,16,128]{3,2,1,0:T(8,128)} %param.13) | copy-start | bytes 24580
  104.7 16.2 %copy-start.1 = (f32[3,64,1,16,127]{4,1,3,0,2:T(8,128)}, f32[3,64,1,16,127]{4,1,3,0,2:T(8,128)S(1)}, u32[]{:S(2)}) copy-start(f32[3,64,1,16,127]{4,1,3,0,2:T(8,128)S(1)} %fusion.2) | copy-start | bytes 4681732
  120.9 4.1 copy-start.5
  287.9 22.5 %collective-permute-start.3 = (f32[3,64,1,16,128]{4,1,3,0,2:T(8,128)S(1)}, f32[3,64,1,16,128]{4,1,3,0,2:T(8,128)S(1)}, u32[]{:S(2)}, u32[]{:S(2)}) collective-permute-start(f32[3,64,1,16,128]{4,1,3,0,2:T(8,128)S(1)} %bitcast.257), channel_id=1, source_target_pairs={{1,0},{2,1},{3,2},{4,3},{5,4},{6,5},{7,6},{8,7},{9,8},{10,9},{11,1... | collective-permute-start | bytes 4718600 | tf_op jit(solution)/shard_map/ppermute | solution.py:26
  289.2 22.7 %collective-permute-start.4 = (f32[3,64,1,16,128]{4,1,3,0,2:T(8,128)S(1)}, f32[3,64,1,16,128]{4,1,3,0,2:T(8,128)S(1)}, u32[]{:S(2)}, u32[]{:S(2)}) collective-permute-start(f32[3,64,1,16,128]{4,1,3,0,2:T(8,128)S(1)} %bitcast.258), channel_id=1, source_target_pairs={{0,1},{1,2},{2,3},{3,4},{4,5},{5,6},{6,7},{7,8},{8,9},{9,10},{10,1... | collective-permute-start | bytes 4718600 | tf_op jit(solution)/shard_map/ppermute | solution.py:24
  294.0 17.9 %copy-start.4 = (f32[3,64,1,15,128]{4,1,3,0,2:T(8,128)}, f32[3,64,1,15,128]{4,1,3,0,2:T(8,128)S(1)}, u32[]{:S(2)}) copy-start(f32[3,64,1,15,128]{4,1,3,0,2:T(8,128)S(1)} %fusion.48) | copy-start | bytes 4423684
  294.5 17.4 %copy-start.2 = (f32[3,64,1,16,127]{4,1,3,0,2:T(8,128)}, f32[3,64,1,16,127]{4,1,3,0,2:T(8,128)S(1)}, u32[]{:S(2)}) copy-start(f32[3,64,1,16,127]{4,1,3,0,2:T(8,128)S(1)} %fusion.1) | copy-start | bytes 4681732
  310.3 1.5 copy-start.6
  311.9 1.1 copy-start.7
  477.8 22.3 %collective-permute-start.5 = (f32[3,64,1,16,128]{4,1,3,0,2:T(8,128)S(1)}, f32[3,64,1,16,128]{4,1,3,0,2:T(8,128)S(1)}, u32[]{:S(2)}, u32[]{:S(2)}) collective-permute-start(f32[3,64,1,16,128]{4,1,3,0,2:T(8,128)S(1)} %bitcast.248), channel_id=1, source_target_pairs={{1,0},{2,1},{3,2},{4,3},{5,4},{6,5},{7,6},{8,7},{9,8},{10,9},{11,1... | collective-permute-start | bytes 4718600 | tf_op jit(solution)/shard_map/ppermute | solution.py:26
  479.1 22.5 %collective-permute-start.6 = (f32[3,64,1,16,128]{4,1,3,0,2:T(8,128)S(1)}, f32[3,64,1,16,128]{4,1,3,0,2:T(8,128)}, u32[]{:S(2)}, u32[]{:S(2)}) collective-permute-start(f32[3,64,1,16,128]{4,1,3,0,2:T(8,128)S(1)} %bitcast.249), channel_id=1, source_target_pairs={{0,1},{1,2},{2,3},{3,4},{4,5},{5,6},{6,7},{7,8},{8,9},{9,10},{10,1... | collective-permute-start | bytes 4718600 | tf_op jit(solution)/shard_map/ppermute | solution.py:24
  504.1 10.3 %collective-permute-start.7 = (f32[3,64,1,4,128]{4,1,3,0,2:T(8,128)S(1)}, f32[3,64,1,4,128]{4,1,3,0,2:T(8,128)S(1)}, u32[]{:S(2)}, u32[]{:S(2)}) collective-permute-start(f32[3,64,1,4,128]{4,1,3,0,2:T(8,128)S(1)} %constant_dynamic-slice_fusion), channel_id=1, source_target_pairs={{0,16},{16,32},{32,48},{48,64},{64,80},{80,96},{96,112},{112,128},... | collective-permute-start | bytes 1179656 | tf_op jit(solution)/shard_map/ppermute | solution.py:13
where the time goes:
time: 588 us
  blocking collectives  430 us (73%)
  waiting for transfers between devices  54.9 us (9%)
  other arithmetic  44.1 us (8%)
  matrix products  30.6 us (5%)
  starting transfers between devices  23.1 us (4%)
    psum x3, blocking collectives, normalize(): gram_b = lax.psum(gram_of(values, b_weight * values), 'dom')  214 us
    psum x2, blocking collectives, on_device(): rayleigh = lax.psum(gram_of(ortho, image), 'dom')  144 us
    psum x1, blocking collectives, on_device(): lax.psum((gram_of(deflate, image), gram_of(deflate[:, :, :, :OV], neighbo...  72.7 us
    ppermute x3, waiting for transfers between devices, with_halo(): lax.ppermute(head, axis, [((i + 1) % count, i) for i in range(ends)])  30.5 us
    ppermute x2, waiting for transfers between devices, from_behind(): lax.ppermute(value, axis, [(source, source + steps) for source in range(l...  21.4 us
    another operation x9, other arithmetic, inverse_factor(): factor = jnp.linalg.cholesky(gram_b)  19.6 us
    dot_general x5, matrix products, mix_cols(): jnp.einsum('ckyxz,kl->clyxz', values, matrix, precision=lax.Precision.HIG...  16.7 us
    another operation x6, other arithmetic, inverse_factor(): lax.linalg.triangular_solve(factor, identity, left_side=True, lower=True)  16.6 us
  transfers between devices with their start and end apart: 8, of which 6 were waited for; matrix products, arithmetic and copies ran while one was open for 1% of the time, Pallas kernels for 0%

commit v1 on v0

--- a/solution.py
+++ b/solution.py
@@ -120,7 +120,7 @@
     for repeat in range(STEPS):
         ortho = normalize(vectors)
         image = operate(ortho)
-        rayleigh = lax.psum(gram_of(ortho, image), "dom")
+        rayleigh = jnp.sum(lax.all_gather(gram_of(ortho, image), "dom"), axis=0)
         residual = image - mix_cols(b_weight * ortho, rayleigh)
         vectors = ortho - 0.5 * residual / diagonal[None, None]
     deflate = unity[None, None] * normalize(vectors)

time: 588 us -> 497 us (0.85)
  blocking collectives: 430 us -> 339 us
    psum x2 -> x0, blocking collectives: 144 us -> none  [on_device(): rayleigh = lax.psum(gram_of(ortho, image), 'dom')]
    all_gather x0 -> x2, blocking collectives: none -> 47.3 us  [on_device(): rayleigh = jnp.sum(lax.all_gather(gram_of(ortho, image), 'dom'), axis=0)]
where the time goes in v1:
time: 497 us; the launch traced here: 496 us
  blocking collectives  339 us (68%)
  waiting for transfers between devices  54.8 us (11%)
  other arithmetic  44.2 us (9%)
  matrix products  30.4 us (6%)
  starting transfers between devices  23.4 us (5%)
    psum x3, blocking collectives, normalize(): gram_b = lax.psum(gram_of(values, b_weight * values), 'dom')  219 us
    psum x1, blocking collectives, on_device(): lax.psum((gram_of(deflate, image), gram_of(deflate[:, :, :, :OV], neighbo...  72.7 us
    all_gather x2, blocking collectives, on_device(): rayleigh = jnp.sum(lax.all_gather(gram_of(ortho, image), 'dom'), axis=0)  47.3 us
    ppermute x3, waiting for transfers between devices, with_halo(): lax.ppermute(head, axis, [((i + 1) % count, i) for i in range(ends)])  30.7 us
    ppermute x2, waiting for transfers between devices, from_behind(): lax.ppermute(value, axis, [(source, source + steps) for source in range(l...  21.3 us
    another operation x9, other arithmetic, inverse_factor(): factor = jnp.linalg.cholesky(gram_b)  19.6 us
    dot_general x5, matrix products, mix_cols(): jnp.einsum('ckyxz,kl->clyxz', values, matrix, precision=lax.Precision.HIG...  17 us
    another operation x6, other arithmetic, inverse_factor(): lax.linalg.triangular_solve(factor, identity, left_side=True, lower=True)  16.6 us
  transfers between devices with their start and end apart: 8, of which 6 were waited for; matrix products, arithmetic and copies ran while one was open for 1% of the time, Pallas kernels for 0%

profile of v1, /device:TPU:128, one launch (start us, length us, event | category | flops | bytes accessed | tf_op | source)
XLA Modules:
  0.0 496.1 jit_solution(17293580408716420935)
XLA Ops:
  1.3 0.8 fusion.104
  2.1 1.7 bitcast_multiply_fusion.1
  3.8 0.1 copy-done
  4.0 0.3 multiply_bitcast_fusion.1
  4.3 2.2 fusion.50
  6.5 74.6 %psum.35 = f32[64,64]{0,1:T(8,128)S(1)} all-reduce(f32[64,64]{0,1:T(8,128)S(1)} %fusion.50), channel_id=1, replica_groups=mesh['sub'=16,'dom'=16] {'dom'}, use_global_device_ids=true, to_apply=%region_0.1 | all-reduce | flops 4096 | bytes 32768 | tf_op jit(solution)/shard_map/psum | solution.py:117
  81.1 0.1 copy.22
  81.2 5.8 %cholesky.59 = f32[64,64]{1,0:T(8,128)S(1)} custom-call(f32[64,64]{1,0:T(8,128)S(1)} %fusion.98), custom_call_target="Cholesky" | custom-call | tf_op jit(solution)/shard_map/jit(cholesky)/cholesky | solution.py:42
  87.1 0.6 compare_reduce_fusion.2
  87.7 0.7 fusion.88
  88.4 4.9 custom-call.7
  93.3 0.3 convolution_bitcast_fusion.3
  93.6 1.9 fusion.32
  95.4 1.3 collective-permute-start
  96.7 5.7 %collective-permute-start.2 = (f32[3,64,1,16,128]{4,1,3,0,2:T(8,128)S(1)}, f32[3,64,1,16,128]{4,1,3,0,2:T(8,128)}, u32[]{:S(2)}, u32[]{:S(2)}) collective-permute-start(f32[3,64,1,16,128]{4,1,3,0,2:T(8,128)S(1)} %bitcast.252), channel_id=1, source_target_pairs={{0,1},{1,2},{2,3},{3,4},{4,5},{5,6},{6,7},{7,8},{8,9},{9,10},{10,1... | collective-permute-start | bytes 4718600 | tf_op jit(solution)/shard_map/ppermute | solution.py:24
  102.5 1.3 collective-permute-start.1
  104.0 0.2 fusion.49
  104.2 0.5 fusion.2
  104.8 16.1 %collective-permute-done.1 = f32[1,16,128]{2,1,0:T(8,128)S(1)} collective-permute-done((f32[1,16,128]{2,1,0:T(8,128)S(1)}, f32[1,16,128]{2,1,0:T(8,128)S(1)}, u32[]{:S(2)}, u32[]{:S(2)}) %collective-permute-start.1) | collective-permute-done | bytes 8224 | tf_op jit(solution)/shard_map/ppermute | solution.py:13
  120.9 0.1 fusion.103
  121.0 1.1 copy-done.5
  122.1 3.5 fusion.65
  125.7 23.6 %all-gather = f32[1024,64]{1,0:T(8,128)S(1)} all-gather(f32[64,64]{1,0:T(8,128)S(1)} %fusion.65), channel_id=2, replica_groups=mesh['sub'=16,'dom'=16] {'dom'}, dimensions={0}, use_global_device_ids=true | all-gather | bytes 278528 | tf_op jit(solution)/shard_map/all_gather | solution.py:123
  149.4 6.2 %fusion.12 = f32[3,64,1,16,128]{4,1,3,0,2:T(8,128)S(1)} fusion(f32[16,128]{1,0:T(8,128)S(1)} %fusion.103, f32[16,128]{1,0:T(8,128)S(1)} %fusion.104, f32[64,64]{1,0:T(8,128)S(1)} %reduce_sum.18, f32[64,3,16,128]{3,0,2,1:T(8,128)S(1)} %fusion.32, f32[3,64,1,16,127]{4,1,3,0,2:T(8,128)} %copy-done.1, f32[3,64,1,15,128]{4,1,3,0,2:T(8,128)} %copy-done.3, ...), kind=kOutput, calls=%fused_computation.17 | convolution fusion | flops 307494912 | bytes 9375744 | tf_op jit(solution)/shard_map/ckyxz,kl->clyxz/dot_general | solution.py:38
  155.5 1.4 fusion.55
  157.0 72.1 %psum.36 = f32[64,64]{0,1:T(8,128)S(1)} all-reduce(f32[64,64]{0,1:T(8,128)S(1)} %fusion.55), channel_id=1, replica_groups=mesh['sub'=16,'dom'=16] {'dom'}, use_global_device_ids=true, to_apply=%region_4.7 | all-reduce | flops 4096 | bytes 32768 | tf_op jit(solution)/shard_map/psum | solution.py:117
  229.2 5.8 %cholesky.70 = f32[64,64]{1,0:T(8,128)S(1)} custom-call(f32[64,64]{1,0:T(8,128)S(1)} %fusion.95), custom_call_target="Cholesky" | custom-call | tf_op jit(solution)/shard_map/jit(cholesky)/cholesky | solution.py:42
  235.0 0.6 compare_reduce_fusion.1
  235.7 0.7 fusion.89
  236.3 4.9 custom-call.8
  241.2 0.3 convolution_bitcast_fusion.2
  241.5 1.5 fusion.26
  243.0 1.3 collective-permute-start.3
  244.3 4.6 collective-permute-start.4
  249.0 0.2 fusion.48
  249.2 0.5 fusion.1
  249.6 16.1 %collective-permute-done.3 = f32[3,64,1,16,128]{4,1,3,0,2:T(8,128)S(1)} collective-permute-done((f32[3,64,1,16,128]{4,1,3,0,2:T(8,128)S(1)}, f32[3,64,1,16,128]{4,1,3,0,2:T(8,128)S(1)}, u32[]{:S(2)}, u32[]{:S(2)}) %collective-permute-start.3) | collective-permute-done | bytes 1572896 | tf_op jit(solution)/shard_map/ppermute | solution.py:26
  265.7 1.3 collective-permute-done.4
  267.1 2.2 fusion.70
  269.3 23.6 %all-gather.1 = f32[1024,64]{1,0:T(8,128)S(1)} all-gather(f32[64,64]{1,0:T(8,128)S(1)} %fusion.70), channel_id=3, replica_groups=mesh['sub'=16,'dom'=16] {'dom'}, dimensions={0}, use_global_device_ids=true | all-gather | bytes 278528 | tf_op jit(solution)/shard_map/all_gather | solution.py:123
  293.0 6.0 %fusion.7 = f32[3,64,1,16,128]{4,1,3,0,2:T(8,128)S(1)} fusion(f32[16,128]{1,0:T(8,128)S(1)} %fusion.103, f32[16,128]{1,0:T(8,128)S(1)} %fusion.104, f32[64,64]{1,0:T(8,128)S(1)} %reduce_sum.19, f32[64,3,16,128]{3,0,2,1:T(8,128)S(1)} %fusion.26, f32[3,64,1,16,127]{4,1,3,0,2:T(8,128)} %copy-done.2, f32[3,64,1,15,128]{4,1,3,0,2:T(8,128)} %copy-done.4, ...), kind=kOutput, calls=%fused_computation.11 | convolution fusion | flops 307494912 | bytes 9375744 | tf_op jit(solution)/shard_map/ckyxz,kl->clyxz/dot_general | solution.py:38
  298.9 1.4 fusion.60
  300.4 72.0 %psum.37 = f32[64,64]{0,1:T(8,128)S(1)} all-reduce(f32[64,64]{0,1:T(8,128)S(1)} %fusion.60), channel_id=1, replica_groups=mesh['sub'=16,'dom'=16] {'dom'}, use_global_device_ids=true, to_apply=%region_6.9 | all-reduce | flops 4096 | bytes 32768 | tf_op jit(solution)/shard_map/psum | solution.py:117
  372.4 0.1 copy.29
  372.5 5.8 %cholesky.81 = f32[64,64]{1,0:T(8,128)S(1)} custom-call(f32[64,64]{1,0:T(8,128)S(1)} %fusion.92), custom_call_target="Cholesky" | custom-call | tf_op jit(solution)/shard_map/jit(cholesky)/cholesky | solution.py:42
  378.4 0.6 compare_reduce_fusion
  379.0 0.7 fusion.90
  379.7 4.9 custom-call.9
  384.6 0.3 convolution_bitcast_fusion.1
  384.8 1.5 bitcast_multiply_fusion
  386.4 1.3 collective-permute-start.5
  387.7 5.7 %collective-permute-start.6 = (f32[3,64,1,16,128]{4,1,3,0,2:T(8,128)S(1)}, f32[3,64,1,16,128]{4,1,3,0,2:T(8,128)}, u32[]{:S(2)}, u32[]{:S(2)}) collective-permute-start(f32[3,64,1,16,128]{4,1,3,0,2:T(8,128)S(1)} %bitcast.247), channel_id=1, source_target_pairs={{0,1},{1,2},{2,3},{3,4},{4,5},{5,6},{6,7},{7,8},{8,9},{9,10},{10,1... | collective-permute-start | bytes 4718600 | tf_op jit(solution)/shard_map/ppermute | solution.py:24
  393.4 0.2 fusion.47
  393.5 0.5 fusion
  394.0 14.6 %collective-permute-done.5 = f32[3,64,1,16,128]{4,1,3,0,2:T(8,128)S(1)} collective-permute-done((f32[3,64,1,16,128]{4,1,3,0,2:T(8,128)S(1)}, f32[3,64,1,16,128]{4,1,3,0,2:T(8,128)S(1)}, u32[]{:S(2)}, u32[]{:S(2)}) %collective-permute-start.5) | collective-permute-done | bytes 1572896 | tf_op jit(solution)/shard_map/ppermute | solution.py:26
  408.7 1.5 collective-permute-done.6
  410.1 2.5 subtract_add_fusion
  412.7 2.2 collective-permute-start.7
  414.9 0.1 convert_bitcast_fusion
  415.0 1.4 copy.30
  416.4 1.4 fusion.75
  417.8 5.2 %collective-permute-done.7 = f32[3,64,1,4,128]{4,1,3,0,2:T(8,128)S(1)} collective-permute-done((f32[3,64,1,4,128]{4,1,3,0,2:T(8,128)S(1)}, f32[3,64,1,4,128]{4,1,3,0,2:T(8,128)S(1)}, u32[]{:S(2)}, u32[]{:S(2)}) %collective-permute-start.7) | collective-permute-done | bytes 393248 | tf_op jit(solution)/shard_map/ppermute | solution.py:13
  423.0 0.5 convolution_bitcast_fusion
  423.4 72.7 %all-reduce.14 = (f32[1,64,64]{2,1,0:T(8,128)}, f32[1,64,64]{2,1,0:T(8,128)}) all-reduce(f32[1,64,64]{2,1,0:T(8,128)S(1)} %fusion.75, f32[1,64,64]{2,1,0:T(8,128)S(1)} %convolution_bitcast_fusion), channel_id=1, replica_groups=mesh['sub'=16,'dom'=16] {'dom'}, use_global_device_ids=true, to_apply=%region_7.10 | all-reduce | flops 8192 | bytes 65536 | tf_op jit(solution)/shard_map/psum | solution.py:130
  (45 shorter events, 0.7 us)
Async XLA Ops:
  2.1 1.9 copy-start
  93.5 8.9 %copy-start.8 = (f32[1,1,16,128]{3,2,1,0:T(8,128)S(1)}, f32[1,1,16,128]{3,2,1,0:T(8,128)}, u32[]{:S(2)}) copy-start(f32[1,1,16,128]{3,2,1,0:T(8,128)} %param.11) | copy-start | bytes 24580
  93.5 10.3 %copy-start.10 = (f32[1,1,16,128]{3,2,1,0:T(8,128)S(1)}, f32[1,1,16,128]{3,2,1,0:T(8,128)}, u32[]{:S(2)}) copy-start(f32[1,1,16,128]{3,2,1,0:T(8,128)} %param.12) | copy-start | bytes 24580
  93.6 10.4 %copy-start.11 = (f32[1,1,16,128]{3,2,1,0:T(8,128)S(1)}, f32[1,1,16,128]{3,2,1,0:T(8,128)}, u32[]{:S(2)}) copy-start(f32[1,1,16,128]{3,2,1,0:T(8,128)} %param.10) | copy-start | bytes 24580
  95.4 25.5 %collective-permute-start = (f32[3,64,1,16,128]{4,1,3,0,2:T(8,128)S(1)}, f32[3,64,1,16,128]{4,1,3,0,2:T(8,128)S(1)}, u32[]{:S(2)}, u32[]{:S(2)}) collective-permute-start(f32[3,64,1,16,128]{4,1,3,0,2:T(8,128)S(1)} %bitcast.251), channel_id=1, source_target_pairs={{1,0},{2,1},{3,2},{4,3},{5,4},{6,5},{7,6},{8,7},{9,8},{10,9},{11,1... | collective-permute-start | bytes 4718600 | tf_op jit(solution)/shard_map/ppermute | solution.py:26
  96.7 24.3 %collective-permute-start.2 = (f32[3,64,1,16,128]{4,1,3,0,2:T(8,128)S(1)}, f32[3,64,1,16,128]{4,1,3,0,2:T(8,128)}, u32[]{:S(2)}, u32[]{:S(2)}) collective-permute-start(f32[3,64,1,16,128]{4,1,3,0,2:T(8,128)S(1)} %bitcast.252), channel_id=1, source_target_pairs={{0,1},{1,2},{2,3},{3,4},{4,5},{5,6},{6,7},{7,8},{8,9},{9,10},{10,1... | collective-permute-start | bytes 4718600 | tf_op jit(solution)/shard_map/ppermute | solution.py:24
  102.5 18.4 %collective-permute-start.1 = (f32[1,16,128]{2,1,0:T(8,128)S(1)}, f32[1,16,128]{2,1,0:T(8,128)S(1)}, u32[]{:S(2)}, u32[]{:S(2)}) collective-permute-start(f32[1,16,128]{2,1,0:T(8,128)S(1)} %bitcast_multiply_fusion.3), channel_id=1, source_target_pairs={{0,1},{1,2},{2,3},{3,4},{4,5},{5,6},{6,7},{7,8},{8,9},{9,10},{10,1... | collective-permute-start | bytes 24584 | tf_op jit(solution)/shard_map/ppermute | solution.py:13
  104.2 16.8 %copy-start.3 = (f32[3,64,1,15,128]{4,1,3,0,2:T(8,128)}, f32[3,64,1,15,128]{4,1,3,0,2:T(8,128)S(1)}, u32[]{:S(2)}) copy-start(f32[3,64,1,15,128]{4,1,3,0,2:T(8,128)S(1)} %fusion.49) | copy-start | bytes 4423684
  104.2 16.7 %copy-start.9 = (f32[1,1,16,128]{3,2,1,0:T(8,128)S(1)}, f32[1,1,16,128]{3,2,1,0:T(8,128)}, u32[]{:S(2)}) copy-start(f32[1,1,16,128]{3,2,1,0:T(8,128)} %param.13) | copy-start | bytes 24580
  104.7 21.0 %copy-start.1 = (f32[3,64,1,16,127]{4,1,3,0,2:T(8,128)}, f32[3,64,1,16,127]{4,1,3,0,2:T(8,128)S(1)}, u32[]{:S(2)}) copy-start(f32[3,64,1,16,127]{4,1,3,0,2:T(8,128)S(1)} %fusion.2) | copy-start | bytes 4681732
  121.0 1.1 copy-start.5
  243.0 22.7 %collective-permute-start.3 = (f32[3,64,1,16,128]{4,1,3,0,2:T(8,128)S(1)}, f32[3,64,1,16,128]{4,1,3,0,2:T(8,128)S(1)}, u32[]{:S(2)}, u32[]{:S(2)}) collective-permute-start(f32[3,64,1,16,128]{4,1,3,0,2:T(8,128)S(1)} %bitcast.255), channel_id=1, source_target_pairs={{1,0},{2,1},{3,2},{4,3},{5,4},{6,5},{7,6},{8,7},{9,8},{10,9},{11,1... | collective-permute-start | bytes 4718600 | tf_op jit(solution)/shard_map/ppermute | solution.py:26
  244.3 22.7 %collective-permute-start.4 = (f32[3,64,1,16,128]{4,1,3,0,2:T(8,128)S(1)}, f32[3,64,1,16,128]{4,1,3,0,2:T(8,128)S(1)}, u32[]{:S(2)}, u32[]{:S(2)}) collective-permute-start(f32[3,64,1,16,128]{4,1,3,0,2:T(8,128)S(1)} %bitcast.256), channel_id=1, source_target_pairs={{0,1},{1,2},{2,3},{3,4},{4,5},{5,6},{6,7},{7,8},{8,9},{9,10},{10,1... | collective-permute-start | bytes 4718600 | tf_op jit(solution)/shard_map/ppermute | solution.py:24
  249.1 17.9 %copy-start.4 = (f32[3,64,1,15,128]{4,1,3,0,2:T(8,128)}, f32[3,64,1,15,128]{4,1,3,0,2:T(8,128)S(1)}, u32[]{:S(2)}) copy-start(f32[3,64,1,15,128]{4,1,3,0,2:T(8,128)S(1)} %fusion.48) | copy-start | bytes 4423684
  249.6 19.6 %copy-start.2 = (f32[3,64,1,16,127]{4,1,3,0,2:T(8,128)}, f32[3,64,1,16,127]{4,1,3,0,2:T(8,128)S(1)}, u32[]{:S(2)}) copy-start(f32[3,64,1,16,127]{4,1,3,0,2:T(8,128)S(1)} %fusion.1) | copy-start | bytes 4681732
  265.7 3.5 copy-start.6
  267.1 2.2 copy-start.7
  386.4 22.3 %collective-permute-start.5 = (f32[3,64,1,16,128]{4,1,3,0,2:T(8,128)S(1)}, f32[3,64,1,16,128]{4,1,3,0,2:T(8,128)S(1)}, u32[]{:S(2)}, u32[]{:S(2)}) collective-permute-start(f32[3,64,1,16,128]{4,1,3,0,2:T(8,128)S(1)} %bitcast.246), channel_id=1, source_target_pairs={{1,0},{2,1},{3,2},{4,3},{5,4},{6,5},{7,6},{8,7},{9,8},{10,9},{11,1... | collective-permute-start | bytes 4718600 | tf_op jit(solution)/shard_map/ppermute | solution.py:26
  387.7 22.5 %collective-permute-start.6 = (f32[3,64,1,16,128]{4,1,3,0,2:T(8,128)S(1)}, f32[3,64,1,16,128]{4,1,3,0,2:T(8,128)}, u32[]{:S(2)}, u32[]{:S(2)}) collective-permute-start(f32[3,64,1,16,128]{4,1,3,0,2:T(8,128)S(1)} %bitcast.247), channel_id=1, source_target_pairs={{0,1},{1,2},{2,3},{3,4},{4,5},{5,6},{6,7},{7,8},{8,9},{9,10},{10,1... | collective-permute-start | bytes 4718600 | tf_op jit(solution)/shard_map/ppermute | solution.py:24
  412.7 10.3 %collective-permute-start.7 = (f32[3,64,1,4,128]{4,1,3,0,2:T(8,128)S(1)}, f32[3,64,1,4,128]{4,1,3,0,2:T(8,128)S(1)}, u32[]{:S(2)}, u32[]{:S(2)}) collective-permute-start(f32[3,64,1,4,128]{4,1,3,0,2:T(8,128)S(1)} %constant_dynamic-slice_fusion), channel_id=1, source_target_pairs={{0,16},{16,32},{32,48},{48,64},{64,80},{80,96},{96,112},{112,128},... | collective-permute-start | bytes 1179656 | tf_op jit(solution)/shard_map/ppermute | solution.py:13
